TPU v7x, 256 devices: a whole 4x4x8 slice. The times are simulated.
256 devices in a mesh: row: 32 (over y, z), col: 8 (over x, core).
Axes of the slice: x: 4, y: 4, z: 8, core: 2. Of those that a mesh axis runs over, the one named last changes fastest.
Arguments:
- query_acts: bfloat16 [256, 8192], P('col', 'row'), may hold values from -6 to 6
- query_grads: bfloat16 [256, 28672], P('row', 'col'), may hold values from -6 to 6
- ritz_mats: float32 [3, 8192, 28672], P(None, 'row', 'col'), may hold values from -0.095683193 to 0.095683193, as said below
- eigenvalues: float32 [3], replicated, may hold values from 0.5 to 4
- train_acts: bfloat16 [256, 8192], P('row'), may hold values from -6 to 6
- train_grads: bfloat16 [256, 28672], P('row', 'col'), may hold values from -6 to 6
Outputs:
- response: bfloat16 [256, 28672], P('row', 'col')
- scores: float32 [256], P('row')
Inputs may be any that keep to these rules, and one draw needn't show every extreme that they name: `ritz_mats`: real entries of order one over the square root of 8192; every matrix has full rank.
All inputs are finite; a program needn't handle non-finite values.
Results may differ from a plain program's by a relative error of at most 0.0012.
Values may be sent and summed in bfloat16 or wider, within the bound.
A program may use at most 64 MiB of HBM per device.

v0:
```python
import math
import jax
import jax.numpy as jnp
from jax import lax
from jax.sharding import PartitionSpec as P

D_OUT = 28672
QUERY = 256
highest = lax.Precision.HIGHEST


def per_device(query_acts, query_grads, ritz_mats, eigenvalues, train_acts, train_grads):
    acts_all = lax.all_gather(query_acts, "col", axis=0, tiled=True)
    grad_tile = lax.dot_general(
        acts_all,
        lax.all_gather(query_grads, "row", axis=0, tiled=True),
        (((0,), (0,)), ((), ())),
        preferred_element_type=jnp.float32,
    )
    local_terms = jnp.sum(ritz_mats * grad_tile[None], axis=(1, 2))
    coeffs = lax.psum(local_terms, ("row", "col"))
    weights = coeffs / (eigenvalues * math.sqrt(QUERY * D_OUT))
    train_local = lax.all_to_all(train_acts, "row", split_axis=1, concat_axis=0, tiled=True).astype(
        jnp.float32
    )
    combined = jnp.tensordot(weights, ritz_mats, axes=1, precision=highest)
    root_width = math.sqrt(D_OUT)
    response_full = lax.psum_scatter(
        jnp.dot(train_local, combined, precision=highest), "row", scatter_dimension=0, tiled=True
    )
    score_terms = jnp.sum(response_full * train_grads.astype(jnp.float32), axis=1) / root_width
    scores = lax.psum(score_terms, "col")
    response = response_full.astype(jnp.bfloat16)
    return (response, scores)


def solution(mesh):
    in_specs = (
        P("col", "row"),
        P("row", "col"),
        P(None, "row", "col"),
        P(),
        P("row", None),
        P("row", "col"),
    )
    out_specs = (P("row", "col"), P("row"))
    return jax.shard_map(
        per_device, mesh=mesh, in_specs=in_specs, out_specs=out_specs, check_vma=False
    )
```

profile of v0, /device:TPU:1, one launch (start us, length us, event | category | flops | bytes accessed | tf_op | source)
XLA Modules:
  0.0 477.4 jit_solution(8239477549064250648)
XLA Ops:
  7.2 0.0 all-gather.2.cloned.1.call-start
  7.2 0.7 all-gather.2.cloned.1.call-update
  7.9 16.0 %all_gather.6 = bf16[256,256]{1,0:T(8,128)(2,1)S(1)} all-gather(bf16[32,256]{1,0:T(8,128)(2,1)} %param.6), channel_id=1, replica_groups=mesh['row'=32,'col'=8] {'col'}, dimensions={0}, use_global_device_ids=true | all-gather | bytes 147456 | tf_op jit(solution)/shard_map/all_gather | solution.py:13
  23.9 64.0 %all-gather.2.cloned.1.call-done = bf16[256,3584]{1,0:T(8,128)(2,1)} async-done(((bf16[8,3584]{1,0:T(8,128)(2,1)}), bf16[256,3584]{1,0:T(8,128)(2,1)}) %all-gather.2.cloned.1.call-update) | async-done | bytes 1835024 | tf_op jit(solution)/shard_map/all_gather | solution.py:16
  87.9 2.2 fusion.8
  90.1 0.0 copy-start.1
  90.1 5.3 %multiply_reduce_fusion = f32[3]{0:T(128)S(1)} fusion(f32[3,256,3584]{2,1,0:T(8,128)} %param.8, f32[256,3584]{1,0:T(8,128)S(1)} %fusion.8), kind=kLoop, calls=%fused_computation.2 | loop fusion | flops 5505021 | bytes 14680076 | tf_op jit(solution)/shard_map/reduce_sum | solution.py:20
  95.4 5.3 %all-to-all-start = ((bf16[8,32,256]{2,0,1:T(8,128)(2,1)}), bf16[8,32,256]{2,0,1:T(8,128)(2,1)S(1)}, u32[]{:S(2)}, u32[]{:S(2)}) async-start(bf16[8,32,256]{2,0,1:T(8,128)(2,1)} %bitcast.2), calls=%async_computation | async-start | bytes 262144 | tf_op jit(solution)/shard_map/all_to_all | solution.py:23
  100.7 0.0 reduce-scatter.4.cloned.1.call-start
  100.8 80.7 %psum.14 = f32[3]{0:T(128)S(1)} all-reduce(f32[3]{0:T(128)S(1)} %multiply_reduce_fusion), channel_id=1, replica_groups=mesh['row'=32,'col'=8] {'row','col'}, use_global_device_ids=true, to_apply=%region_1.0 | all-reduce | flops 3 | bytes 24 | tf_op jit(solution)/shard_map/psum | solution.py:21
  181.5 0.0 copy-done.1
  181.5 40.2 %fusion = f32[1,256,3584]{2,0,1:T(1,128)} fusion(f32[3,256,3584]{2,1,0:T(8,128)} %param.8, f32[3]{0:T(128)S(1)} %psum.14, f32[3]{0:T(128)S(1)} %copy-done.1), kind=kOutput, calls=%fused_computation | convolution fusion | flops 33030150 | bytes 14680088 | tf_op jit(solution)/shard_map/dot_general | solution.py:26
  221.7 0.0 all-to-all-done
  221.7 6.9 %convolution_bitcast_fusion = f32[256,3584]{0,1:T(8,128)} fusion(f32[1,256,3584]{2,0,1:T(1,128)} %fusion, bf16[8,32,256]{2,0,1:T(8,128)(2,1)S(1)} %all-to-all-done), kind=kOutput, calls=%fused_computation.3 | convolution fusion | flops 2818572288 | bytes 7471104 | tf_op jit(solution)/shard_map/dot_general | solution.py:29
  228.6 5.2 %copy.14 = f32[256,3584]{1,0:T(8,128)} copy(f32[256,3584]{0,1:T(8,128)} %convolution_bitcast_fusion) | data formatting | bytes 7340032
  233.7 0.0 copy-start
  233.7 0.0 reduce-scatter.4.cloned.1.call-update
  233.8 0.8 copy-done
  234.6 0.3 copy.10
  234.9 211.5 %reduce-scatter.4.cloned.1.call-done = f32[8,3584]{1,0:T(8,128)} async-done(((f32[256,3584]{1,0:T(8,128)}), f32[8,3584]{1,0:T(8,128)}) %reduce-scatter.4.cloned.1.call-update) | async-done | bytes 114704
  446.4 2.7 copy.15
  449.1 2.5 multiply_reduce_fusion.1
  451.6 0.9 copy.11
  452.5 18.1 %psum.15 = f32[8]{0:T(128)} all-reduce(f32[8]{0:T(128)S(1)} %broadcast_multiply_fusion), channel_id=1, replica_groups=mesh['row'=32,'col'=8] {'col'}, use_global_device_ids=true, to_apply=%region_4.0 | all-reduce | flops 8 | bytes 64 | tf_op jit(solution)/shard_map/psum | solution.py:32
  (1 shorter events, 0.0 us)
Async XLA Ops:
  7.2 80.8 %all-gather.2.cloned.1.call-start = ((), (), s32[]{:S(2)}) async-start(), calls=%async_computation.2 | async-start | bytes 1892352 | tf_op jit(solution)/shard_map/all_gather | solution.py:16
  90.1 91.4 %copy-start.1 = (f32[3]{0:T(128)S(1)}, f32[3]{0:T(128)}, u32[]{:S(2)}) copy-start(f32[3]{0:T(128)} %param.9) | copy-start | bytes 40
  95.4 126.3 %all-to-all-start = ((bf16[8,32,256]{2,0,1:T(8,128)(2,1)}), bf16[8,32,256]{2,0,1:T(8,128)(2,1)S(1)}, u32[]{:S(2)}, u32[]{:S(2)}) async-start(bf16[8,32,256]{2,0,1:T(8,128)(2,1)} %bitcast.2), calls=%async_computation | async-start | bytes 262144 | tf_op jit(solution)/shard_map/all_to_all | solution.py:23
  100.7 345.7 %reduce-scatter.4.cloned.1.call-start = ((), (), s32[]{:S(2)}) async-start(), calls=%async_computation.3 | async-start | bytes 3784704
  233.7 0.8 copy-start
Sparse Core Ops, SparseCore 0:
  10.6 77.3 all-gather.1
  233.9 212.4 reduce-scatter.3
where the time goes:
time: 478 us; the launch traced here: 477 us
  waiting for transfers between devices  276 us (58%)
  blocking collectives  115 us (24%)
  matrix products  49.2 us (10%)
  between operations  14.1 us (3%)
  local copies, waits for them, and re-layouts  9.87 us (2%)
  other arithmetic  7.81 us (2%)
  starting transfers between devices  5.4 us (1%)
    unnamed x3, waiting for transfers between devices  212 us
    psum x1, blocking collectives, per_device(): coeffs = lax.psum(local_terms, ('row', 'col'))  80.7 us
    all_gather x1, waiting for transfers between devices, per_device(): lax.all_gather(query_grads, 'row', axis=0, tiled=True)  64 us
    dot_general x1, matrix products, per_device(): combined = jnp.tensordot(weights, ritz_mats, axes=1, precision=highest)  40.2 us
    psum x1, blocking collectives, per_device(): scores = lax.psum(score_terms, 'col')  18.1 us
    all_gather x1, blocking collectives, per_device(): acts_all = lax.all_gather(query_acts, 'col', axis=0, tiled=True)  16 us
    unnamed x7, local copies, waits for them, and re-layouts  9.57 us
  transfers between devices with their start and end apart: 3, of which 2 were waited for; matrix products, arithmetic and copies ran while one was open for 8% of the time, Pallas kernels for 0%

commit v1 on v0

--- a/solution.py
+++ b/solution.py
@@ -9,11 +9,18 @@
 highest = lax.Precision.HIGHEST
 
 
+def _process_zone(local_x):
+    front = lax.axis_size("row")
+    low = jnp.stack([local_x] * front, axis=0)
+    item_now = lax.all_to_all(low, "row", split_axis=0, concat_axis=0)
+    return jnp.concatenate(item_now, axis=0)
+
+
 def per_device(query_acts, query_grads, ritz_mats, eigenvalues, train_acts, train_grads):
     acts_all = lax.all_gather(query_acts, "col", axis=0, tiled=True)
     grad_tile = lax.dot_general(
         acts_all,
-        lax.all_gather(query_grads, "row", axis=0, tiled=True),
+        _process_zone(query_grads),
         (((0,), (0,)), ((), ())),
         preferred_element_type=jnp.float32,
     )

time: 478 us -> 451 us (0.944)
  waiting for transfers between devices: 276 us -> 240 us
  starting transfers between devices: 5.4 us -> 18.7 us
  blocking collectives: 115 us -> 110 us
    all_gather x1 -> x0, waiting for transfers between devices: 64 us -> none  [per_device(): lax.all_gather(query_grads, 'row', axis=0, tiled=True)]
    all_to_all x0 -> x1, waiting for transfers between devices: none -> 29.5 us  [_process_zone(): item_now = lax.all_to_all(low, 'row', split_axis=0, concat_axis=0)]
    all_to_all x0 -> x1, starting transfers between devices: none -> 12 us  [_process_zone(): item_now = lax.all_to_all(low, 'row', split_axis=0, concat_axis=0)]
    unnamed x3 -> x2, waiting for transfers between devices: 212 us -> 211 us
    unnamed x7 -> x9, local copies, waits for them, and re-layouts: 9.57 us -> 9.57 us
  transfers between devices with their start and end apart: 3 -> 3, of which waited for: 2 -> 2; matrix products, arithmetic and copies ran while one was open for 8% -> 9% of each run, Pallas kernels for 0% -> 0%
where the time goes in v1:
time: 451 us
  waiting for transfers between devices  240 us (53%)
  blocking collectives  110 us (24%)
  matrix products  47.7 us (11%)
  starting transfers between devices  18.7 us (4%)
  between operations  14.1 us (3%)
  local copies, waits for them, and re-layouts  12.1 us (3%)
  other arithmetic  7.81 us (2%)
    unnamed x2, waiting for transfers between devices  211 us
    psum x1, blocking collectives, per_device(): coeffs = lax.psum(local_terms, ('row', 'col'))  77.7 us
    dot_general x1, matrix products, per_device(): combined = jnp.tensordot(weights, ritz_mats, axes=1, precision=highest)  40.2 us
    all_to_all x1, waiting for transfers between devices, _process_zone(): item_now = lax.all_to_all(low, 'row', split_axis=0, concat_axis=0)  29.5 us
    psum x1, blocking collectives, per_device(): scores = lax.psum(score_terms, 'col')  18.1 us
    all_gather x1, blocking collectives, per_device(): acts_all = lax.all_gather(query_acts, 'col', axis=0, tiled=True)  13.9 us
    all_to_all x1, starting transfers between devices, _process_zone(): item_now = lax.all_to_all(low, 'row', split_axis=0, concat_axis=0)  12 us
    unnamed x9, local copies, waits for them, and re-layouts  9.57 us
  transfers between devices with their start and end apart: 3, of which 2 were waited for; matrix products, arithmetic and copies ran while one was open for 9% of the time, Pallas kernels for 0%

profile of v1, /device:TPU:1, one launch (start us, length us, event | category | flops | bytes accessed | tf_op | source)
XLA Modules:
  0.0 450.5 jit_solution(10153347538467698464)
XLA Ops:
  7.2 0.0 copy-start.1
  7.2 2.2 stack.2
  9.4 12.0 %all-to-all-start = ((bf16[32,8,3584]{2,1,0:T(8,128)(2,1)}), bf16[32,8,3584]{2,1,0:T(8,128)(2,1)S(1)}, u32[]{:S(2)}, u32[]{:S(2)}) async-start(bf16[32,8,3584]{2,1,0:T(8,128)(2,1)} %stack.2), calls=%async_computation | async-start | bytes 3670016 | tf_op jit(solution)/shard_map/all_to_all | solution.py:15
  21.4 0.0 copy-done.1
  21.4 13.9 %all_gather.3 = bf16[256,256]{1,0:T(8,128)(2,1)S(1)} all-gather(bf16[32,256]{1,0:T(8,128)(2,1)S(1)} %copy-done.1), channel_id=1, replica_groups=mesh['row'=32,'col'=8] {'col'}, dimensions={0}, use_global_device_ids=true | all-gather | bytes 147456 | tf_op jit(solution)/shard_map/all_gather | solution.py:20
  35.3 29.5 %all-to-all-done = bf16[32,8,3584]{2,1,0:T(8,128)(2,1)S(1)} async-done(((bf16[32,8,3584]{2,1,0:T(8,128)(2,1)}), bf16[32,8,3584]{2,1,0:T(8,128)(2,1)S(1)}, u32[]{:S(2)}, u32[]{:S(2)}) %all-to-all-start) | async-done | bytes 1835040 | tf_op jit(solution)/shard_map/all_to_all | solution.py:15
  64.8 0.7 fusion.4
  65.5 0.0 copy-start.2
  65.5 5.3 %multiply_reduce_fusion = f32[3]{0:T(128)S(1)} fusion(f32[3,256,3584]{2,1,0:T(8,128)} %param.8, f32[256,3584]{1,0:T(8,128)S(1)} %fusion.4), kind=kLoop, calls=%fused_computation.2 | loop fusion | flops 5505021 | bytes 14680076 | tf_op jit(solution)/shard_map/reduce_sum | solution.py:27
  70.8 6.7 %all-to-all-start.1 = ((bf16[8,32,256]{2,0,1:T(8,128)(2,1)}), bf16[8,32,256]{2,0,1:T(8,128)(2,1)S(1)}, u32[]{:S(2)}, u32[]{:S(2)}) async-start(bf16[8,32,256]{2,0,1:T(8,128)(2,1)} %bitcast.3), calls=%async_computation.1 | async-start | bytes 262144 | tf_op jit(solution)/shard_map/all_to_all | solution.py:30
  77.4 0.0 reduce-scatter.4.cloned.1.call-start
  77.5 77.7 %psum.14 = f32[3]{0:T(128)S(1)} all-reduce(f32[3]{0:T(128)S(1)} %multiply_reduce_fusion), channel_id=1, replica_groups=mesh['row'=32,'col'=8] {'row','col'}, use_global_device_ids=true, to_apply=%region_1.0 | all-reduce | flops 3 | bytes 24 | tf_op jit(solution)/shard_map/psum | solution.py:28
  155.1 40.2 %fusion = f32[1,256,3584]{2,0,1:T(1,128)} fusion(f32[3,256,3584]{2,1,0:T(8,128)} %param.8, f32[3]{0:T(128)S(1)} %psum.14, f32[3]{0:T(128)S(1)} %copy-done.2), kind=kOutput, calls=%fused_computation | convolution fusion | flops 33030150 | bytes 14680088 | tf_op jit(solution)/shard_map/dot_general | solution.py:33
  195.3 0.0 all-to-all-done.1
  195.3 6.9 %convolution_bitcast_fusion = f32[256,3584]{0,1:T(8,128)} fusion(f32[1,256,3584]{2,0,1:T(1,128)} %fusion, bf16[8,32,256]{2,0,1:T(8,128)(2,1)S(1)} %all-to-all-done.1), kind=kOutput, calls=%fused_computation.3 | convolution fusion | flops 2818572288 | bytes 7471104 | tf_op jit(solution)/shard_map/dot_general | solution.py:36
  202.2 5.2 %copy.14 = f32[256,3584]{1,0:T(8,128)} copy(f32[256,3584]{0,1:T(8,128)} %convolution_bitcast_fusion) | data formatting | bytes 7340032
  207.4 0.0 reduce-scatter.4.cloned.1.call-update
  207.4 0.8 copy-done
  208.2 0.3 copy.10
  208.5 210.9 %reduce-scatter.4.cloned.1.call-done = f32[8,3584]{1,0:T(8,128)} async-done(((f32[256,3584]{1,0:T(8,128)}), f32[8,3584]{1,0:T(8,128)}) %reduce-scatter.4.cloned.1.call-update) | async-done | bytes 114704
  419.4 2.7 copy.15
  422.1 2.5 multiply_reduce_fusion.1
  424.6 0.9 copy.11
  425.5 18.1 %psum.15 = f32[8]{0:T(128)} all-reduce(f32[8]{0:T(128)S(1)} %broadcast_multiply_fusion), channel_id=1, replica_groups=mesh['row'=32,'col'=8] {'col'}, use_global_device_ids=true, to_apply=%region_4.0 | all-reduce | flops 8 | bytes 64 | tf_op jit(solution)/shard_map/psum | solution.py:39
  (3 shorter events, 0.0 us)
Async XLA Ops:
  7.2 14.2 %copy-start.1 = (bf16[32,256]{1,0:T(8,128)(2,1)S(1)}, bf16[32,256]{1,0:T(8,128)(2,1)}, u32[]{:S(2)}) copy-start(bf16[32,256]{1,0:T(8,128)(2,1)} %param.6) | copy-start | bytes 49156
  9.4 55.4 %all-to-all-start = ((bf16[32,8,3584]{2,1,0:T(8,128)(2,1)}), bf16[32,8,3584]{2,1,0:T(8,128)(2,1)S(1)}, u32[]{:S(2)}, u32[]{:S(2)}) async-start(bf16[32,8,3584]{2,1,0:T(8,128)(2,1)} %stack.2), calls=%async_computation | async-start | bytes 3670016 | tf_op jit(solution)/shard_map/all_to_all | solution.py:15
  65.5 89.7 %copy-start.2 = (f32[3]{0:T(128)S(1)}, f32[3]{0:T(128)}, u32[]{:S(2)}) copy-start(f32[3]{0:T(128)} %param.9) | copy-start | bytes 40
  70.8 124.6 %all-to-all-start.1 = ((bf16[8,32,256]{2,0,1:T(8,128)(2,1)}), bf16[8,32,256]{2,0,1:T(8,128)(2,1)S(1)}, u32[]{:S(2)}, u32[]{:S(2)}) async-start(bf16[8,32,256]{2,0,1:T(8,128)(2,1)} %bitcast.3), calls=%async_computation.1 | async-start | bytes 262144 | tf_op jit(solution)/shard_map/all_to_all | solution.py:30
  77.4 342.0 %reduce-scatter.4.cloned.1.call-start = ((), (), s32[]{:S(2)}) async-start(), calls=%async_computation.3 | async-start | bytes 3784704
  207.4 0.8 copy-start
Sparse Core Ops, SparseCore 0:
  207.5 211.8 reduce-scatter.3
